TPU v7x, 512 devices: a whole 4x8x8 slice. The times are simulated.
512 devices in a mesh: sample: 32 (over z_hi, y, core), space: 16 (over z_lo, x).
Axes of the slice: x: 4, y: 8, z: 8 (z_hi: 2, z_lo: 4; z = z_hi * 4 + z_lo), core: 2. Of those that a mesh axis runs over, the one named last changes fastest.
Arguments:
- volumes: bfloat16 [512, 32, 8192], P('sample', None, 'space'), may hold values from -6 to 6
- grad_out: bfloat16 [512, 128, 1024], P(('sample', 'space')), may hold values from -6 to 6
- kernel_first: bfloat16 [27, 64, 32], replicated, may hold values from -0.21875 to 0.21875
- bias_first: float32 [64], replicated, may hold values from -3 to 3
- kernel_second: bfloat16 [27, 128, 64], replicated, may hold values from -0.15625 to 0.15625
- bias_second: float32 [128], replicated, may hold values from -3 to 3
Outputs:
- features: bfloat16 [512, 128, 1024], P(('sample', 'space'))
- kernel_grad_first: float32 [27, 64, 32], replicated
- bias_grad_first: float32 [64], replicated
- kernel_grad_second: float32 [27, 128, 64], replicated
- bias_grad_second: float32 [128], replicated
All inputs are finite; a program needn't handle non-finite values.
Results may differ from a plain program's by a relative error of at most 0.0085.
The roundings to bfloat16 on the way count: a program that leaves them out, or rounds other values in their place, can miss the bound.
Values may be sent and summed in bfloat16 or wider, within the bound.
A program may use at most 192 MiB of HBM per device.

v0:
```python
import math

import jax
import jax.numpy as jnp
from jax import lax
from jax.experimental import pallas as pl
from jax.experimental.pallas import tpu as pltpu
from jax.sharding import PartitionSpec as P

LEAK_SLOPE = 0.3
BF = jnp.bfloat16
F32 = jnp.float32
MESH = pl.DeviceIdType.MESH
LANES = 128
PARTS = 8
TILES1, ROWS1 = 7, 8
TILES2, ROWS2 = 14, 16


def lane_iota(rows):
    return lax.broadcasted_iota(jnp.int32, (rows, LANES), 1)


def dot(a, b, ca=1, cb=0):
    return lax.dot_general(a, b, (((ca,), (cb,)), ((), ())), preferred_element_type=F32)


def column(row, n):
    r = lax.broadcasted_iota(jnp.int32, (n, n), 0)
    c = lax.broadcasted_iota(jnp.int32, (n, n), 1)
    return jnp.sum(jnp.where(r == c, jnp.broadcast_to(row, (n, n)), 0.0), axis=1, keepdims=True)


def row_of(col, n):
    r = lax.broadcasted_iota(jnp.int32, (n, n), 0)
    c = lax.broadcasted_iota(jnp.int32, (n, n), 1)
    return jnp.sum(jnp.where(r == c, jnp.broadcast_to(col, (n, n)), 0.0), axis=0, keepdims=True)


def tap_masks(rows, side, mirror):
    lane = lane_iota(rows)
    h = (lane // side) % side
    w = lane % side
    out = []
    for t in range(9):
        dh, dw = t // 3 - 1, t % 3 - 1
        if mirror:
            dh, dw = -dh, -dw
        ok = (h + dh >= 0) & (h + dh < side) & (w + dw >= 0) & (w + dw < side)
        mask = jnp.where(ok, 1.0, 0.0).astype(BF) if (dh or dw) else None
        out.append((mask, (-(dh * side + dw)) % LANES))
    return out


def taps_of(x, masks):
    return [x if m is None else pltpu.roll(x, s, 1) * m for m, s in masks]


def pool_matrix(value, transpose):
    shape = (LANES, 4 * LANES) if transpose else (4 * LANES, LANES)
    big = lax.broadcasted_iota(jnp.int32, shape, 1 if transpose else 0)
    small = lax.broadcasted_iota(jnp.int32, shape, 0 if transpose else 1)
    q, lane = big // LANES, big % LANES
    target = (lane // 64) * 64 + q * 16 + ((lane % 64) // 16) * 4 + (lane % 8) // 2
    return jnp.where(target == small, value, 0.0).astype(BF)


def split_pair(pair, lo):
    top, bottom = pair[:32], pair[32:]
    return (
        jnp.where(lo, top, pltpu.roll(bottom, 64, 1)),
        jnp.where(lo, pltpu.roll(top, 64, 1), bottom),
    )


def join_pair(first, second, lo):
    return (
        jnp.where(lo, first, pltpu.roll(second, 64, 1)),
        jnp.where(lo, pltpu.roll(first, 64, 1), second),
    )


def position():
    sample, space = lax.axis_index("sample"), lax.axis_index("space")
    core = sample % 2
    y = (sample // 2) % 8
    z = (sample // 16) * 4 + space // 4
    x = space % 4
    return core, x, y, z


def device(core, x, y, z):
    return ((z // 4) * 16 + y * 2 + core, (z % 4) * 4 + x)


def space_peers():
    sample, space = lax.axis_index("sample"), lax.axis_index("space")
    return [(sample, (space + k) % 16) for k in range(1, 16)]


def all_peers():
    core, x, y, z = position()
    out = space_peers()
    out += [device(core, x, (y + k) % 8, z) for k in range(1, 8)]
    out += [device(core, x, y, (1 - z // 4) * 4 + k) for k in range(4)]
    out += [device(1 - core, x, y, z)]
    return out


def remote(src, dst, ssem, rsem, peer):
    return pltpu.make_async_remote_copy(
        src_ref=src, dst_ref=dst, send_sem=ssem, recv_sem=rsem,
        device_id=peer, device_id_type=MESH,
    )


def exchange(send, recv, ssem, rsem):
    me = lax.axis_index("space")
    copies = []
    for k, peer in enumerate(space_peers()):
        copy = remote(send.at[peer[1]], recv.at[me], ssem.at[k], rsem.at[k], peer)
        copy.start()
        copies.append(copy)
    recv[me] = send[me]
    return copies


class Sum:
    def __init__(self, tiles, rows, kind, refs):
        self.tiles, self.rows, self.kind = tiles, rows, kind
        self.share = -(-tiles // 8)
        (self.g, self.rc, self.xs, self.rx, self.ys, self.ry, self.rz, self.fs, self.ay, self.bx,
         self.out, self.ssem, self.rsem) = refs
        self.pos = core, x, y, z = position()
        self.other = device(1 - core, x, y, z)
        self.xp = [device(core, (x + k) % 4, y, z) for k in range(1, 4)]
        self.yp = [device(core, x, (y + k) % 8, z) for k in range(1, 8)]
        self.zp = [device(core, x, y, (z + k) % 8) for k in range(1, 8)]
        self.started, self.now = [], []

    @staticmethod
    def scratch(tiles, rows, kind):
        share = -(-tiles // 8)
        dims = [
            (PARTS, tiles), (4, tiles), (4, tiles), (3, tiles), (8 * share,), (7, share),
            (8, share), (share,), (8 * share,), (4, tiles), (PARTS, tiles),
        ]
        out = [pltpu.VMEM(d + (rows, LANES), kind) for d in dims]
        return out + [pltpu.SemaphoreType.DMA((29,)), pltpu.SemaphoreType.DMA((29,))]

    def send(self, i, src, dst, peer):
        copy = remote(src, dst, self.ssem.at[i], self.rsem.at[i], peer)
        copy.start()
        self.started.append(copy)
        self.now.append(copy)

    def arrive(self):
        for copy in self.now:
            copy.wait_recv()
        self.now = []

    def mine(self, ref):
        return ref.at[pl.ds(self.pos[2] * self.share, self.share)]

    def step(self, i):
        core, x, y, z = self.pos
        kind = self.kind
        if i == 0:
            self.send(0, self.g.at[pl.ds((1 - core) * 4, 4)], self.rc, self.other)
            return
        self.arrive()
        if i == 1:
            for n in range(4):
                self.xs[n] = (self.g[core * 4 + n].astype(F32) + self.rc[n].astype(F32)).astype(kind)
            for k in range(3):
                self.send(1 + k, self.xs.at[(x + k + 1) % 4], self.rx.at[k], self.xp[k])
        elif i == 2:
            total = self.xs[x].astype(F32)
            for k in range(3):
                total = total + self.rx[k].astype(F32)
            self.ys[0 : self.tiles] = total.astype(kind)
            for k in range(7):
                at = pl.ds(((y + k + 1) % 8) * self.share, self.share)
                self.send(4 + k, self.ys.at[at], self.ry.at[k], self.yp[k])
        elif i == 3:
            total = self.ys[pl.ds(y * self.share, self.share)].astype(F32)
            for k in range(7):
                total = total + self.ry[k].astype(F32)
            self.fs[...] = total.astype(kind)
            self.rz[z] = total.astype(kind)
            for k in range(7):
                self.send(11 + k, self.fs, self.rz.at[z], self.zp[k])
        elif i == 4:
            total = self.rz[0].astype(F32)
            for k in range(1, 8):
                total = total + self.rz[k].astype(F32)
            self.ay[pl.ds(y * self.share, self.share)] = total.astype(kind)
            for k in range(7):
                self.send(18 + k, self.mine(self.ay), self.mine(self.ay), self.yp[k])
        elif i == 5:
            for k in range(3):
                self.send(25 + k, self.ay.at[0 : self.tiles], self.bx.at[x], self.xp[k])
            self.bx[x] = self.ay[0 : self.tiles]
        elif i == 6:
            self.send(28, self.bx, self.out.at[pl.ds(core * 4, 4)], self.other)
            for n in range(4):
                self.out[core * 4 + n] = self.bx[n]

    def finish(self):
        for copy in self.started:
            copy.wait_send()


def put_taps(x, masks, s9, s, j):
    for t, y in enumerate(taps_of(x, masks)):
        s9[s, 32 * t : 32 * t + 32, LANES * j : LANES * j + LANES] = y


def inner_taps(vol, s9, masks, lo):
    @pl.loop(0, 4)
    def _(t):
        at = pl.ds(pl.multiple_of(t * LANES, LANES), LANES)
        for j in range(8):
            a, b = vol[2 * j, :, at], vol[2 * j + 1, :, at]
            put_taps(jnp.where(lo, a, pltpu.roll(b, 64, 1)), masks, s9, 2 * t + 1, j)
            put_taps(jnp.where(lo, pltpu.roll(a, 64, 1), b), masks, s9, 2 * t + 2, j)


def outer_taps(before, after, s9, masks, lo):
    for j in range(8):
        a, b = before[2 * j], before[2 * j + 1]
        put_taps(jnp.where(lo, pltpu.roll(a, 64, 1), b), masks, s9, 0, j)
        a, b = after[2 * j], after[2 * j + 1]
        put_taps(jnp.where(lo, a, pltpu.roll(b, 64, 1)), masks, s9, 9, j)


def first_outputs(part, b1, keep, yb, send, lo):
    bias = column(b1[...], 64)

    @pl.loop(0, 4)
    def _(q):
        total = None
        for r in range(2):
            p = 2 * q + r
            pre = part[p, 0:64] + part[p + 1, 64:128] + part[p + 2, 128:192] + bias
            positive = pre > 0
            keep[p] = jnp.where(positive, 1.0, 0.0).astype(BF)
            act = jnp.where(positive, pre, LEAK_SLOPE * pre)
            total = act if total is None else total + act
        high = total.astype(BF)
        low = (total - high.astype(F32)).astype(BF)
        at = pl.ds(pl.multiple_of(q * LANES, LANES), LANES)
        for j in range(8):
            cut = slice(LANES * j, LANES * j + LANES)
            yb[LANES * j : LANES * j + 64, at] = high[:, cut]
            yb[LANES * j + 64 : LANES * j + LANES, at] = low[:, cut]

    z = dot(yb[...], pool_matrix(0.125, False))
    for j in range(8):
        pooled = z[LANES * j : LANES * j + 64] + z[LANES * j + 64 : LANES * j + LANES]
        one, two = split_pair(pooled, lo)
        send[2 * j] = one.astype(BF)
        send[2 * j + 1] = two.astype(BF)


def shift_planes(x, by):
    lane = lax.broadcasted_iota(jnp.int32, x.shape, 1)
    zero = jnp.zeros_like(x)
    if by > 0:
        return jnp.where(lane < 16, zero, pltpu.roll(x, 16, 1))
    return jnp.where(lane >= 1008, zero, pltpu.roll(x, 1008, 1))


def second_layer(recv, w2, wb, b2, grad, features, send, d3, s9b, d9, lo):
    forward = tap_masks(64, 4, False)
    for i in range(8):
        cut = slice(LANES * i, LANES * i + LANES)
        top, bottom = join_pair(recv[2 * i], recv[2 * i + 1], lo)
        x = jnp.concatenate([top, bottom], axis=0)
        for t, y in enumerate(taps_of(x, forward)):
            s9b[64 * t : 64 * t + 64, cut] = y
    p3 = dot(w2[...], s9b[...])
    second = shift_planes(p3[0:128], 1) + p3[128:256] + shift_planes(p3[256:384], -1)
    second = second + column(b2[...], 128)
    positive = second > 0
    features[...] = jnp.where(positive, second, LEAK_SLOPE * second).astype(BF)
    delta = (grad[...].astype(F32) * jnp.where(positive, 1.0, LEAK_SLOPE)).astype(BF)
    d3[128:256] = delta

    backward = tap_masks(128, 4, True)
    for i in range(8):
        cut = slice(LANES * i, LANES * i + LANES)
        for t, y in enumerate(taps_of(delta[:, cut], backward)):
            d9[128 * t : 128 * t + 128, cut] = y
    r3 = dot(wb[...], d9[...])
    spread = shift_planes(r3[0:64], -1) + r3[64:128] + shift_planes(r3[128:192], 1)
    for i in range(8):
        one, two = split_pair(spread[:, LANES * i : LANES * i + LANES], lo)
        send[2 * i] = one.astype(BF)
        send[2 * i + 1] = two.astype(BF)


def second_taps(d3, s9b, acc2, g2):
    delta = d3[128:256]
    d3[0:128] = shift_planes(delta, -1)
    d3[256:384] = shift_planes(delta, 1)
    acc2[...] = dot(s9b[...], d3[...], 1, 1)
    for a in range(3):
        for r in range(36):
            t = 36 * a + r
            tile = acc2[16 * r : 16 * r + 16, LANES * a : LANES * a + LANES]
            g2[t // TILES2, t % TILES2] = tile.astype(BF)
    for t in range(108, PARTS * TILES2):
        g2[t // TILES2, t % TILES2] = jnp.zeros((ROWS2, LANES), BF)
    return row_of(jnp.sum(delta.astype(F32), axis=1, keepdims=True), 128)


def first_deltas(recv, keep, tt, dr, lo):
    for j in range(8):
        top, bottom = join_pair(recv[2 * j], recv[2 * j + 1], lo)
        tt[64 * j : 64 * j + 32] = top
        tt[64 * j + 32 : 64 * j + 64] = bottom
    for i in (0, 1, 10, 11):
        dr[i] = jnp.zeros((64, 1024), BF)
    spread_to = pool_matrix(1.0, True)
    total = jnp.zeros((64, LANES), F32)
    for q in range(4):
        u = dot(tt[...], spread_to[:, LANES * q : LANES * q + LANES])
        for r in range(2):
            p = 2 * q + r
            for j in range(8):
                cut = slice(LANES * j, LANES * j + LANES)
                slope = jnp.where(keep[p, :, cut] > 0, 1.0, LEAK_SLOPE).astype(F32)
                delta = (u[64 * j : 64 * j + 64] * 0.125 * slope).astype(BF)
                dr[9 - p, :, cut] = delta
                total = total + delta.astype(F32)
    return row_of(jnp.sum(total, axis=1, keepdims=True), 64)


def first_taps(s9, dr, acc1, first, last):
    acc = None
    for s in range(first, last):
        term = dot(s9[s], dr[9 - s : 12 - s].reshape(192, 1024), 1, 1)
        acc = term if acc is None else acc + term
    if first == 0:
        acc1[:, 0:192] = acc
    else:
        acc1[:, 0:192] += acc


def pack_first(acc1, bias1, bias2, g1):
    lo = lane_iota(8) < 64
    row = lax.broadcasted_iota(jnp.int32, (8, LANES), 0)

    def put(t, value):
        g1[t // TILES1, t % TILES1] = value

    for k in range(36):
        put(k, acc1[8 * k : 8 * k + 8, 0:LANES])
    for k in range(18):
        left = acc1[8 * k : 8 * k + 8, LANES:256]
        right = acc1[144 + 8 * k : 152 + 8 * k, LANES:256]
        put(36 + k, jnp.where(lo, left, pltpu.roll(right, 64, 1)))
    one = jnp.concatenate([bias1, jnp.zeros((1, 64), F32)], axis=1)
    one = jnp.broadcast_to(one, (8, LANES))
    two = jnp.broadcast_to(bias2, (8, LANES))
    put(54, jnp.where(row == 0, one, jnp.where(row == 1, two, 0.0)))
    put(55, jnp.zeros((8, LANES), F32))


def unpack_first(c, out1, outb):
    def get(t):
        return c[t // TILES1, t % TILES1]

    def put(a, r, value):
        out1[9 * a + r // 4, 8 * (r % 4) : 8 * (r % 4) + 8] = value

    for k in range(36):
        put(0, k, get(k)[:, 0:64])
        put(1, k, get(k)[:, 64:128])
    for k in range(18):
        put(2, k, get(36 + k)[:, 0:64])
        put(2, 18 + k, get(36 + k)[:, 64:128])
    outb[...] = get(54)


def step_kernel(
    vol_in, k1_in, b1, k2_in, b2, grad_in, feat_out, out1, out2, outb,
    vol, k1, k2, grad, feat, before, after, s9, part, keep, w1, yb, send1, recv1,
    w2, wb, s9b, d3, d9, acc2, send2, recv2, tt, dr, acc1,
    lsem, hssem, hrsem, s1, r1, s2, r2, *sums,
):
    space = lax.axis_index("space")
    sample = lax.axis_index("sample")
    n = len(sums) // 2
    sum1 = Sum(TILES1, ROWS1, F32, sums[:n])
    sum2 = Sum(TILES2, ROWS2, BF, sums[n:])
    peers = all_peers()
    barrier = pltpu.get_barrier_semaphore()
    for peer in peers:
        pl.semaphore_signal(barrier, inc=1, device_id=peer, device_id_type=MESH)
    loads = [
        pltpu.make_async_copy(src, dst, lsem.at[i])
        for i, (src, dst) in enumerate(((vol_in, vol), (k1_in, k1), (k2_in, k2), (grad_in.at[0], grad)))
    ]
    for load in loads:
        load.start()

    lo = lane_iota(32) < 64
    masks = tap_masks(32, 8, False)
    loads[0].wait()
    inner_taps(vol, s9, masks, lo)
    loads[1].wait()
    for a in range(3):
        w1[64 * a : 64 * a + 64] = jnp.transpose(k1[9 * a : 9 * a + 9].reshape(288, 64))

    pl.semaphore_wait(barrier, len(peers))
    tail = remote(vol.at[:, :, pl.ds(384, 128)], before, hssem.at[0], hrsem.at[0], (sample, (space + 1) % 16))
    head = remote(vol.at[:, :, pl.ds(0, 128)], after, hssem.at[1], hrsem.at[1], (sample, (space + 15) % 16))

    @pl.when(space < 15)
    def _():
        tail.start()

    @pl.when(space > 0)
    def _():
        head.start()

    @pl.when(space == 0)
    def _():
        before[...] = jnp.zeros_like(before)

    @pl.when(space == 15)
    def _():
        after[...] = jnp.zeros_like(after)

    for s in range(1, 9):
        part[s] = dot(w1[...], s9[s])

    @pl.when(space > 0)
    def _():
        tail.wait_recv()
        head.wait_send()

    @pl.when(space < 15)
    def _():
        head.wait_recv()
        tail.wait_send()

    outer_taps(before, after, s9, masks, lo)
    for s in (0, 9):
        part[s] = dot(w1[...], s9[s])
    first_outputs(part, b1, keep, yb, send1, lo)
    there = exchange(send1, recv1, s1, r1)

    loads[2].wait()
    for a in range(3):
        w2[128 * a : 128 * a + 128] = jnp.transpose(k2[9 * a : 9 * a + 9].reshape(576, 128))
        for t in range(9):
            wb[64 * a : 64 * a + 64, 128 * t : 128 * t + 128] = k2[9 * a + t]
    loads[3].wait()
    for copy in there:
        copy.wait_recv()
    second_layer(recv1, w2, wb, b2, grad, feat, send2, d3, s9b, d9, lo)
    back = exchange(send2, recv2, s2, r2)
    write = pltpu.make_async_copy(feat, feat_out.at[0], lsem.at[4])
    write.start()

    bias2 = second_taps(d3, s9b, acc2, sum2.g)
    for total in (sum1, sum2):
        pad = 8 * total.share - total.tiles
        total.ys[total.tiles : 8 * total.share] = jnp.zeros((pad, total.rows, LANES), total.kind)
    sum2.step(0)
    for copy in back:
        copy.wait_recv()
    sum2.step(1)
    bias1 = first_deltas(recv2, keep, tt, dr, lo)
    first_taps(s9, dr, acc1, 0, 3)
    sum2.step(2)
    first_taps(s9, dr, acc1, 3, 10)
    pack_first(acc1, bias1, bias2, sum1.g)
    sum1.step(0)
    sum2.step(3)
    sum1.step(1)
    sum1.step(2)
    sum2.step(4)
    sum1.step(3)
    sum2.step(5)
    sum1.step(4)
    sum2.step(6)
    sum1.step(5)
    sum2.step(7)
    out2[...] = sum2.out[...]
    sum1.step(6)
    sum1.step(7)
    unpack_first(sum1.out, out1, outb)
    for copy in there + back:
        copy.wait_send()
    sum1.finish()
    sum2.finish()
    write.wait()


def shape(dims, kind=BF):
    return jax.ShapeDtypeStruct(dims, kind)


def on_device(volumes, grad_out, kernel_first, bias_first, kernel_second, bias_second):
    devices = lax.axis_size("sample") * lax.axis_size("space")
    scale_one = 1.0 / math.sqrt(volumes.shape[0] * volumes.shape[2] * devices)
    scale_two = 1.0 / math.sqrt(grad_out.shape[0] * grad_out.shape[2] * devices)
    vmem = pl.BlockSpec(memory_space=pltpu.VMEM)
    anywhere = pl.BlockSpec(memory_space=pl.ANY)
    dma = pltpu.SemaphoreType.DMA
    feat, out1, out2, outb = pl.pallas_call(
        step_kernel,
        name="step",
        out_shape=[
            shape((1, 128, 1024)), shape((27, 32, 64), F32),
            shape((PARTS, TILES2, ROWS2, LANES)), shape((8, LANES), F32),
        ],
        in_specs=[anywhere, anywhere, vmem, anywhere, vmem, anywhere],
        out_specs=[anywhere, vmem, vmem, vmem],
        scratch_shapes=[
            pltpu.VMEM((16, 32, 512), BF),
            pltpu.VMEM((27, 32, 64), BF),
            pltpu.VMEM((27, 64, 128), BF),
            pltpu.VMEM((128, 1024), BF),
            pltpu.VMEM((128, 1024), BF),
            pltpu.VMEM((16, 32, LANES), BF),
            pltpu.VMEM((16, 32, LANES), BF),
            pltpu.VMEM((10, 288, 1024), BF),
            pltpu.VMEM((10, 192, 1024), F32),
            pltpu.VMEM((8, 64, 1024), BF),
            pltpu.VMEM((192, 288), BF),
            pltpu.VMEM((1024, 512), BF),
            pltpu.VMEM((16, 32, LANES), BF),
            pltpu.VMEM((16, 32, LANES), BF),
            pltpu.VMEM((384, 576), BF),
            pltpu.VMEM((192, 1152), BF),
            pltpu.VMEM((576, 1024), BF),
            pltpu.VMEM((384, 1024), BF),
            pltpu.VMEM((1152, 1024), BF),
            pltpu.VMEM((576, 384), F32),
            pltpu.VMEM((16, 32, LANES), BF),
            pltpu.VMEM((16, 32, LANES), BF),
            pltpu.VMEM((512, LANES), BF),
            pltpu.VMEM((12, 64, 1024), BF),
            pltpu.VMEM((288, 256), F32),
            dma((5,)), dma((2,)), dma((2,)), dma((15,)), dma((15,)), dma((15,)), dma((15,)),
        ]
        + Sum.scratch(TILES1, ROWS1, F32)
        + Sum.scratch(TILES2, ROWS2, BF),
        compiler_params=pltpu.CompilerParams(
            vmem_limit_bytes=56 << 20, collective_id=0, has_side_effects=True
        ),
    )(
        volumes, jnp.swapaxes(kernel_first, 1, 2), bias_first.reshape(1, -1),
        jnp.swapaxes(kernel_second, 1, 2), bias_second.reshape(1, -1), grad_out,
    )
    taps1 = jnp.swapaxes(out1 * scale_one, 1, 2)
    taps2 = out2.reshape(-1, LANES)[: 27 * 64].astype(F32) * scale_two
    taps2 = jnp.swapaxes(taps2.reshape(27, 64, LANES), 1, 2)
    return feat, taps1, outb[0, :64] * scale_one, taps2, outb[1] * scale_two


def solution(mesh):
    in_specs = (P("sample", None, "space"), P(("sample", "space"), None, None), P(), P(), P(), P())
    out_specs = (P(("sample", "space"), None, None), P(), P(), P(), P())
    return jax.shard_map(
        on_device, mesh=mesh, in_specs=in_specs, out_specs=out_specs, check_vma=False
    )
```

profile of v0, /device:TPU:1, one launch (start us, length us, event | category | flops | bytes accessed | tf_op | source)
XLA Modules:
  0.0 82.3 jit_solution(17370615335335364833)
XLA Ops:
  0.6 75.7 %step.1 = (bf16[1,128,1024]{2,1,0:T(8,128)(2,1)}, f32[27,32,64]{2,1,0:T(8,128)}, bf16[8,14,16,128]{3,2,1,0:T(8,128)(2,1)}, f32[8,128]{1,0:T(8,128)}) custom-call(bf16[16,32,512]{2,1,0:T(8,128)(2,1)} %vol_in.1, bf16[27,32,64]{2,1,0:T(8,128)(2,1)} %bitcast.17, f32[1,64]{1,0:T(1,128)} %bitcast.18, bf16[27,64,128]{2,1,0:T(8,128)(2,1)} %bitcast.15, ...), custom_call_target="tpu_custom_call" | custom-call | tf_op jit(solution)/shard_map/step/pallas_call | solution.py:515
  76.3 0.0 copy-start
  76.3 1.2 %multiply_bitcast_fusion.1 = f32[128]{0:T(128)} fusion(f32[8,128]{1,0:T(8,128)} %get-tuple-element.11), kind=kLoop, calls=%fused_computation.2 | loop fusion | flops 128 | bytes 1024 | tf_op jit(solution)/shard_map/mul | solution.py:564
  77.6 1.2 %multiply_bitcast_fusion.2 = f32[64]{0:T(128)} fusion(f32[8,128]{1,0:T(8,128)} %get-tuple-element.11), kind=kLoop, calls=%fused_computation.3 | loop fusion | flops 64 | bytes 512 | tf_op jit(solution)/shard_map/mul | solution.py:564
  78.8 1.8 %multiply_bitcast_fusion = f32[27,64,32]{1,2,0:T(8,128)} fusion(f32[27,32,64]{2,1,0:T(8,128)} %get-tuple-element.10), kind=kLoop, calls=%fused_computation.1 | loop fusion | flops 55296 | bytes 442368 | tf_op jit(solution)/shard_map/transpose | solution.py:561
  80.6 0.0 copy-done
  80.6 0.0 copy-start.1
  80.6 1.0 %convert_multiply_fusion = f32[1728,128]{1,0:T(8,128)} fusion(bf16[1792,128]{1,0:T(8,128)(2,1)S(1)} %bitcast.16), kind=kLoop, calls=%fused_computation | loop fusion | flops 442368 | bytes 1327104 | tf_op jit(solution)/shard_map/mul | solution.py:562
  81.6 0.0 copy-done.1
  81.6 0.7 copy.12
Async XLA Ops:
  76.3 4.2 %copy-start = (bf16[8,14,16,128]{3,2,1,0:T(8,128)(2,1)S(1)}, bf16[8,14,16,128]{3,2,1,0:T(8,128)(2,1)}, u32[]{:S(2)}) copy-start(bf16[8,14,16,128]{3,2,1,0:T(8,128)(2,1)} %get-tuple-element.12) | copy-start | bytes 1376260
  80.6 1.0 %copy-start.1 = (bf16[1,128,1024]{2,1,0:T(8,128)(2,1)S(1)}, bf16[1,128,1024]{2,1,0:T(8,128)(2,1)}, u32[]{:S(2)}) copy-start(bf16[1,128,1024]{2,1,0:T(8,128)(2,1)} %get-tuple-element.18) | copy-start | bytes 786436
where the time goes:
time: 82.5 us; the launch traced here: 82.3 us
  Pallas kernels  75.7 us (92%)
  other arithmetic  5.21 us (6%)
    pallas_call x1, Pallas kernels, on_device(): pl.pallas_call(step_kernel, name='step', out_shape=[shape((1, 128, 1024))...  75.7 us
    mul x2, other arithmetic, on_device(): return (feat, taps1, outb[0, :64] * scale_one, taps2, outb[1] * scale_two)  2.42 us
    transpose x1, other arithmetic, on_device(): taps1 = jnp.swapaxes(out1 * scale_one, 1, 2)  1.81 us

commit v1 on v0

--- a/solution.py
+++ b/solution.py
@@ -1,3 +1,4 @@
+import functools
 import math
 
 import jax
@@ -368,24 +369,44 @@
     put(55, jnp.zeros((8, LANES), F32))
 
 
-def unpack_first(c, out1, outb):
+def finish_kernel(
+    scale_one, scale_two, feat_in, c1_in, c2_in, feat_out, out1, out2, outb1, outb2, feat, c1, c2, sem
+):
+    loads = [
+        pltpu.make_async_copy(src, dst, sem.at[i])
+        for i, (src, dst) in enumerate(((c2_in, c2), (c1_in, c1), (feat_in, feat)))
+    ]
+    for load in loads:
+        load.start()
+    loads[0].wait()
+
     def get(t):
-        return c[t // TILES1, t % TILES1]
+        return c1[t // TILES1, t % TILES1] * scale_one
 
     def put(a, r, value):
         out1[9 * a + r // 4, 8 * (r % 4) : 8 * (r % 4) + 8] = value
 
+    for t in range(108):
+        tile = c2[t // TILES2, t % TILES2].astype(F32) * scale_two
+        out2[t // 4, 16 * (t % 4) : 16 * (t % 4) + 16] = tile
+    loads[1].wait()
     for k in range(36):
-        put(0, k, get(k)[:, 0:64])
-        put(1, k, get(k)[:, 64:128])
+        tile = get(k)
+        put(0, k, tile[:, 0:64])
+        put(1, k, tile[:, 64:128])
     for k in range(18):
-        put(2, k, get(36 + k)[:, 0:64])
-        put(2, 18 + k, get(36 + k)[:, 64:128])
-    outb[...] = get(54)
+        tile = get(36 + k)
+        put(2, k, tile[:, 0:64])
+        put(2, 18 + k, tile[:, 64:128])
+    tile = c1[54 // TILES1, 54 % TILES1]
+    outb1[...] = tile[0:1, 0:64] * scale_one
+    outb2[...] = tile[1:2] * scale_two
+    loads[2].wait()
+    feat_out[0] = feat[...]
 
 
 def step_kernel(
-    vol_in, k1_in, b1, k2_in, b2, grad_in, feat_out, out1, out2, outb,
+    vol_in, k1_in, b1, k2_in, b2, grad_in, feat_out, out1, out2,
     vol, k1, k2, grad, feat, before, after, s9, part, keep, w1, yb, send1, recv1,
     w2, wb, s9b, d3, d9, acc2, send2, recv2, tt, dr, acc1,
     lsem, hssem, hrsem, s1, r1, s2, r2, *sums,
@@ -463,25 +484,29 @@
         copy.wait_recv()
     second_layer(recv1, w2, wb, b2, grad, feat, send2, d3, s9b, d9, lo)
     back = exchange(send2, recv2, s2, r2)
-    write = pltpu.make_async_copy(feat, feat_out.at[0], lsem.at[4])
-    write.start()
+
+    writes = [
+        pltpu.make_async_copy(src, dst, lsem.at[4 + i])
+        for i, (src, dst) in enumerate(((feat, feat_out), (sum2.out, out2), (sum1.out, out1)))
+    ]
+    writes[0].start()
 
     bias2 = second_taps(d3, s9b, acc2, sum2.g)
     for total in (sum1, sum2):
         pad = 8 * total.share - total.tiles
         total.ys[total.tiles : 8 * total.share] = jnp.zeros((pad, total.rows, LANES), total.kind)
     sum2.step(0)
+    sum2.step(1)
     for copy in back:
         copy.wait_recv()
-    sum2.step(1)
     bias1 = first_deltas(recv2, keep, tt, dr, lo)
-    first_taps(s9, dr, acc1, 0, 3)
+    first_taps(s9, dr, acc1, 0, 7)
     sum2.step(2)
-    first_taps(s9, dr, acc1, 3, 10)
+    first_taps(s9, dr, acc1, 7, 10)
     pack_first(acc1, bias1, bias2, sum1.g)
     sum1.step(0)
+    sum1.step(1)
     sum2.step(3)
-    sum1.step(1)
     sum1.step(2)
     sum2.step(4)
     sum1.step(3)
@@ -490,15 +515,16 @@
     sum2.step(6)
     sum1.step(5)
     sum2.step(7)
-    out2[...] = sum2.out[...]
+    writes[1].start()
     sum1.step(6)
     sum1.step(7)
-    unpack_first(sum1.out, out1, outb)
+    writes[2].start()
     for copy in there + back:
         copy.wait_send()
     sum1.finish()
     sum2.finish()
-    write.wait()
+    for write in writes:
+        write.wait()
 
 
 def shape(dims, kind=BF):
@@ -510,17 +536,17 @@
     scale_one = 1.0 / math.sqrt(volumes.shape[0] * volumes.shape[2] * devices)
     scale_two = 1.0 / math.sqrt(grad_out.shape[0] * grad_out.shape[2] * devices)
     vmem = pl.BlockSpec(memory_space=pltpu.VMEM)
-    anywhere = pl.BlockSpec(memory_space=pl.ANY)
+    anywhere = pl.BlockSpec(memory_space=pltpu.HBM)
     dma = pltpu.SemaphoreType.DMA
-    feat, out1, out2, outb = pl.pallas_call(
+    feat, sums1, sums2 = pl.pallas_call(
         step_kernel,
         name="step",
         out_shape=[
-            shape((1, 128, 1024)), shape((27, 32, 64), F32),
-            shape((PARTS, TILES2, ROWS2, LANES)), shape((8, LANES), F32),
+            shape((128, 1024)), shape((PARTS, TILES1, ROWS1, LANES), F32),
+            shape((PARTS, TILES2, ROWS2, LANES)),
         ],
         in_specs=[anywhere, anywhere, vmem, anywhere, vmem, anywhere],
-        out_specs=[anywhere, vmem, vmem, vmem],
+        out_specs=[anywhere] * 3,
         scratch_shapes=[
             pltpu.VMEM((16, 32, 512), BF),
             pltpu.VMEM((27, 32, 64), BF),
@@ -547,7 +573,7 @@
             pltpu.VMEM((512, LANES), BF),
             pltpu.VMEM((12, 64, 1024), BF),
             pltpu.VMEM((288, 256), F32),
-            dma((5,)), dma((2,)), dma((2,)), dma((15,)), dma((15,)), dma((15,)), dma((15,)),
+            dma((7,)), dma((2,)), dma((2,)), dma((15,)), dma((15,)), dma((15,)), dma((15,)),
         ]
         + Sum.scratch(TILES1, ROWS1, F32)
         + Sum.scratch(TILES2, ROWS2, BF),
@@ -558,10 +584,25 @@
         volumes, jnp.swapaxes(kernel_first, 1, 2), bias_first.reshape(1, -1),
         jnp.swapaxes(kernel_second, 1, 2), bias_second.reshape(1, -1), grad_out,
     )
-    taps1 = jnp.swapaxes(out1 * scale_one, 1, 2)
-    taps2 = out2.reshape(-1, LANES)[: 27 * 64].astype(F32) * scale_two
-    taps2 = jnp.swapaxes(taps2.reshape(27, 64, LANES), 1, 2)
-    return feat, taps1, outb[0, :64] * scale_one, taps2, outb[1] * scale_two
+    feat, out1, out2, outb1, outb2 = pl.pallas_call(
+        functools.partial(finish_kernel, scale_one, scale_two),
+        name="finish",
+        out_shape=[
+            shape((1, 128, 1024)), shape((27, 32, 64), F32), shape((27, 64, 128), F32),
+            shape((1, 64), F32), shape((1, 128), F32),
+        ],
+        in_specs=[anywhere] * 3,
+        out_specs=[vmem] * 5,
+        scratch_shapes=[
+            pltpu.VMEM((128, 1024), BF),
+            pltpu.VMEM((PARTS, TILES1, ROWS1, LANES), F32),
+            pltpu.VMEM((PARTS, TILES2, ROWS2, LANES), BF),
+            dma((3,)),
+        ],
+        compiler_params=pltpu.CompilerParams(vmem_limit_bytes=56 << 20),
+    )(feat, sums1, sums2)
+    out1, out2 = jnp.swapaxes(out1, 1, 2), jnp.swapaxes(out2, 1, 2)
+    return feat, out1, outb1.reshape(-1), out2, outb2.reshape(-1)
 
 
 def solution(mesh):

time: 82.5 us -> 73.1 us (0.89)
  other arithmetic: 5.21 us -> 0 us
  Pallas kernels: 75.7 us -> 72.3 us
    pallas_call x1 -> x2, Pallas kernels: 75.7 us -> 72.3 us  [the longest x1 69.9 us: on_device(): pl.pallas_call(step_kernel, name='step', out_shape=[shape((128, 1024)), s...]
    mul x3 -> x0, other arithmetic: 3.4 us -> none  [the longest x2 2.42 us: on_device(): return (feat, taps1, outb[0, :64] * scale_one, taps2, outb[1] * scale_two)]
    transpose x1 -> x0, other arithmetic: 1.81 us -> none  [on_device(): taps1 = jnp.swapaxes(out1 * scale_one, 1, 2)]
where the time goes in v1:
time: 73.1 us; the launch traced here: 72.9 us
  Pallas kernels  72.3 us (99%)
    pallas_call x1, Pallas kernels, on_device(): pl.pallas_call(step_kernel, name='step', out_shape=[shape((128, 1024)), s...  69.9 us
    pallas_call x1, Pallas kernels, on_device(): pl.pallas_call(functools.partial(finish_kernel, scale_one, scale_two), na...  2.39 us

profile of v1, /device:TPU:1, one launch (start us, length us, event | category | flops | bytes accessed | tf_op | source)
XLA Modules:
  0.0 72.9 jit_solution(8185072882376122412)
XLA Ops:
  0.6 69.9 %step.1 = (bf16[128,1024]{1,0:T(8,128)(2,1)}, f32[8,7,8,128]{3,2,1,0:T(8,128)}, bf16[8,14,16,128]{3,2,1,0:T(8,128)(2,1)}) custom-call(bf16[16,32,512]{2,1,0:T(8,128)(2,1)} %vol_in.1, bf16[27,32,64]{2,1,0:T(8,128)(2,1)} %bitcast.9, f32[1,64]{1,0:T(1,128)} %bitcast.10, bf16[27,64,128]{2,1,0:T(8,128)(2,1)} %bitcast.8, f32[1,128]{1,0:T(1,128)} %bitcast.11, ...), custom_call_target="tpu_custom_call" | custom-call | tf_op jit(solution)/shard_map/step/pallas_call | solution.py:541
  70.5 2.4 %finish.1 = (bf16[1,128,1024]{2,1,0:T(8,128)(2,1)}, f32[27,32,64]{2,1,0:T(8,128)}, f32[27,64,128]{2,1,0:T(8,128)}, f32[1,64]{1,0:T(1,128)}, f32[1,128]{1,0:T(1,128)}) custom-call(bf16[128,1024]{1,0:T(8,128)(2,1)} %get-tuple-element.13.feat_in, f32[8,7,8,128]{3,2,1,0:T(8,128)} %get-tuple-element.14.c1_in, bf16[8,14,16,128]{3,2,1,0:T(8,128)(2,1)} %get-tuple-element.15.c2_in), custom_call_target="tpu_custom_call" | custom-call | tf_op jit(solution)/shard_map/finish/pallas_call | solution.py:587

commit v2 on v1

--- a/solution.py
+++ b/solution.py
@@ -14,6 +14,7 @@
 MESH = pl.DeviceIdType.MESH
 LANES = 128
 PARTS = 8
+OTHER_TAPS = (0, 1, 2, 3, 5, 6, 7, 8)
 TILES1, ROWS1 = 7, 8
 TILES2, ROWS2 = 14, 16
 
@@ -212,34 +213,51 @@
             copy.wait_send()
 
 
-def put_taps(x, masks, s9, s, j):
-    for t, y in enumerate(taps_of(x, masks)):
-        s9[s, 32 * t : 32 * t + 32, LANES * j : LANES * j + LANES] = y
-
-
-def inner_taps(vol, s9, masks, lo):
+def fill_shifts(shifts):
+    source = lax.broadcasted_iota(jnp.int32, (LANES, LANES), 0)
+    lane = lane_iota(LANES)
+    h, w = (lane // 8) % 8, lane % 8
+    for k, t in enumerate(OTHER_TAPS):
+        dh, dw = t // 3 - 1, t % 3 - 1
+        ok = (h + dh >= 0) & (h + dh < 8) & (w + dw >= 0) & (w + dw < 8)
+        hit = ok & (source == lane + (8 * dh + dw))
+        shifts[:, LANES * k : LANES * k + LANES] = jnp.where(hit, 1.0, 0.0).astype(BF)
+
+
+def store_taps(rows, shifts, s9, s):
+    moved = dot(rows[...], shifts[...])
+    for j in range(8):
+        at, cut = slice(32 * j, 32 * j + 32), slice(LANES * j, LANES * j + LANES)
+        s9[s, 128:160, cut] = rows[at]
+        for k, t in enumerate(OTHER_TAPS):
+            s9[s, 32 * t : 32 * t + 32, cut] = moved[at, LANES * k : LANES * k + LANES].astype(BF)
+
+
+def inner_taps(vol, s9, xs, shifts, lo):
     @pl.loop(0, 4)
     def _(t):
         at = pl.ds(pl.multiple_of(t * LANES, LANES), LANES)
         for j in range(8):
             a, b = vol[2 * j, :, at], vol[2 * j + 1, :, at]
-            put_taps(jnp.where(lo, a, pltpu.roll(b, 64, 1)), masks, s9, 2 * t + 1, j)
-            put_taps(jnp.where(lo, pltpu.roll(a, 64, 1), b), masks, s9, 2 * t + 2, j)
-
-
-def outer_taps(before, after, s9, masks, lo):
+            xs[0, 32 * j : 32 * j + 32] = jnp.where(lo, a, pltpu.roll(b, 64, 1))
+            xs[1, 32 * j : 32 * j + 32] = jnp.where(lo, pltpu.roll(a, 64, 1), b)
+        store_taps(xs.at[0], shifts, s9, 2 * t + 1)
+        store_taps(xs.at[1], shifts, s9, 2 * t + 2)
+
+
+def outer_taps(before, after, s9, xs, shifts, lo):
     for j in range(8):
         a, b = before[2 * j], before[2 * j + 1]
-        put_taps(jnp.where(lo, pltpu.roll(a, 64, 1), b), masks, s9, 0, j)
+        xs[0, 32 * j : 32 * j + 32] = jnp.where(lo, pltpu.roll(a, 64, 1), b)
         a, b = after[2 * j], after[2 * j + 1]
-        put_taps(jnp.where(lo, a, pltpu.roll(b, 64, 1)), masks, s9, 9, j)
-
-
-def first_outputs(part, b1, keep, yb, send, lo):
+        xs[1, 32 * j : 32 * j + 32] = jnp.where(lo, a, pltpu.roll(b, 64, 1))
+    store_taps(xs.at[0], shifts, s9, 0)
+    store_taps(xs.at[1], shifts, s9, 9)
+
+
+def first_planes(part, b1, keep, yb, qs):
     bias = column(b1[...], 64)
-
-    @pl.loop(0, 4)
-    def _(q):
+    for q in qs:
         total = None
         for r in range(2):
             p = 2 * q + r
@@ -250,12 +268,14 @@
             total = act if total is None else total + act
         high = total.astype(BF)
         low = (total - high.astype(F32)).astype(BF)
-        at = pl.ds(pl.multiple_of(q * LANES, LANES), LANES)
+        at = slice(LANES * q, LANES * q + LANES)
         for j in range(8):
             cut = slice(LANES * j, LANES * j + LANES)
             yb[LANES * j : LANES * j + 64, at] = high[:, cut]
             yb[LANES * j + 64 : LANES * j + LANES, at] = low[:, cut]
 
+
+def first_outputs(yb, send, lo):
     z = dot(yb[...], pool_matrix(0.125, False))
     for j in range(8):
         pooled = z[LANES * j : LANES * j + 64] + z[LANES * j + 64 : LANES * j + LANES]
@@ -406,8 +426,8 @@
 
 
 def step_kernel(
-    vol_in, k1_in, b1, k2_in, b2, grad_in, feat_out, out1, out2,
-    vol, k1, k2, grad, feat, before, after, s9, part, keep, w1, yb, send1, recv1,
+    vol_in, k1_in, b1_in, k2_in, b2_in, grad_in, feat_out, out1, out2,
+    vol, xs, shifts, b1, b2, k1, k2, grad, feat, before, after, s9, part, keep, w1, yb, send1, recv1,
     w2, wb, s9b, d3, d9, acc2, send2, recv2, tt, dr, acc1,
     lsem, hssem, hrsem, s1, r1, s2, r2, *sums,
 ):
@@ -422,18 +442,17 @@
         pl.semaphore_signal(barrier, inc=1, device_id=peer, device_id_type=MESH)
     loads = [
         pltpu.make_async_copy(src, dst, lsem.at[i])
-        for i, (src, dst) in enumerate(((vol_in, vol), (k1_in, k1), (k2_in, k2), (grad_in.at[0], grad)))
+        for i, (src, dst) in enumerate((
+            (vol_in, vol), (k1_in, k1), (k2_in, k2), (grad_in.at[0], grad), (b1_in, b1), (b2_in, b2),
+        ))
     ]
     for load in loads:
         load.start()
 
     lo = lane_iota(32) < 64
-    masks = tap_masks(32, 8, False)
+    fill_shifts(shifts)
     loads[0].wait()
-    inner_taps(vol, s9, masks, lo)
-    loads[1].wait()
-    for a in range(3):
-        w1[64 * a : 64 * a + 64] = jnp.transpose(k1[9 * a : 9 * a + 9].reshape(288, 64))
+    inner_taps(vol, s9, xs, shifts, lo)
 
     pl.semaphore_wait(barrier, len(peers))
     tail = remote(vol.at[:, :, pl.ds(384, 128)], before, hssem.at[0], hrsem.at[0], (sample, (space + 1) % 16))
@@ -455,8 +474,13 @@
     def _():
         after[...] = jnp.zeros_like(after)
 
+    loads[1].wait()
+    loads[4].wait()
+    for a in range(3):
+        w1[64 * a : 64 * a + 64] = jnp.transpose(k1[9 * a : 9 * a + 9].reshape(288, 64))
     for s in range(1, 9):
         part[s] = dot(w1[...], s9[s])
+    first_planes(part, b1, keep, yb, (1, 2))
 
     @pl.when(space > 0)
     def _():
@@ -468,10 +492,11 @@
         head.wait_recv()
         tail.wait_send()
 
-    outer_taps(before, after, s9, masks, lo)
+    outer_taps(before, after, s9, xs, shifts, lo)
     for s in (0, 9):
         part[s] = dot(w1[...], s9[s])
-    first_outputs(part, b1, keep, yb, send1, lo)
+    first_planes(part, b1, keep, yb, (0, 3))
+    first_outputs(yb, send1, lo)
     there = exchange(send1, recv1, s1, r1)
 
     loads[2].wait()
@@ -480,13 +505,14 @@
         for t in range(9):
             wb[64 * a : 64 * a + 64, 128 * t : 128 * t + 128] = k2[9 * a + t]
     loads[3].wait()
+    loads[5].wait()
     for copy in there:
         copy.wait_recv()
     second_layer(recv1, w2, wb, b2, grad, feat, send2, d3, s9b, d9, lo)
     back = exchange(send2, recv2, s2, r2)
 
     writes = [
-        pltpu.make_async_copy(src, dst, lsem.at[4 + i])
+        pltpu.make_async_copy(src, dst, lsem.at[6 + i])
         for i, (src, dst) in enumerate(((feat, feat_out), (sum2.out, out2), (sum1.out, out1)))
     ]
     writes[0].start()
@@ -545,10 +571,14 @@
             shape((128, 1024)), shape((PARTS, TILES1, ROWS1, LANES), F32),
             shape((PARTS, TILES2, ROWS2, LANES)),
         ],
-        in_specs=[anywhere, anywhere, vmem, anywhere, vmem, anywhere],
+        in_specs=[anywhere] * 6,
         out_specs=[anywhere] * 3,
         scratch_shapes=[
             pltpu.VMEM((16, 32, 512), BF),
+            pltpu.VMEM((2, 256, LANES), BF),
+            pltpu.VMEM((LANES, 8 * LANES), BF),
+            pltpu.VMEM((1, 64), F32),
+            pltpu.VMEM((1, 128), F32),
             pltpu.VMEM((27, 32, 64), BF),
             pltpu.VMEM((27, 64, 128), BF),
             pltpu.VMEM((128, 1024), BF),
@@ -573,7 +603,7 @@
             pltpu.VMEM((512, LANES), BF),
             pltpu.VMEM((12, 64, 1024), BF),
             pltpu.VMEM((288, 256), F32),
-            dma((7,)), dma((2,)), dma((2,)), dma((15,)), dma((15,)), dma((15,)), dma((15,)),
+            dma((9,)), dma((2,)), dma((2,)), dma((15,)), dma((15,)), dma((15,)), dma((15,)),
         ]
         + Sum.scratch(TILES1, ROWS1, F32)
         + Sum.scratch(TILES2, ROWS2, BF),

time: 73.1 us -> 69.9 us (0.956)
  Pallas kernels: 72.3 us -> 69.1 us
    pallas_call x1, Pallas kernels: 69.9 us -> 66.7 us  [on_device(): pl.pallas_call(step_kernel, name='step', out_shape=[shape((128, 1024)), s...]
where the time goes in v2:
time: 69.9 us; the launch traced here: 69.8 us
  Pallas kernels  69.1 us (99%)
    pallas_call x1, Pallas kernels, on_device(): pl.pallas_call(step_kernel, name='step', out_shape=[shape((128, 1024)), s...  66.7 us
    pallas_call x1, Pallas kernels, on_device(): pl.pallas_call(functools.partial(finish_kernel, scale_one, scale_two), na...  2.39 us

profile of v2, /device:TPU:1, one launch (start us, length us, event | category | flops | bytes accessed | tf_op | source)
XLA Modules:
  0.0 69.8 jit_solution(16423530885874745866)
XLA Ops:
  0.6 66.7 %step.1 = (bf16[128,1024]{1,0:T(8,128)(2,1)}, f32[8,7,8,128]{3,2,1,0:T(8,128)}, bf16[8,14,16,128]{3,2,1,0:T(8,128)(2,1)}) custom-call(bf16[16,32,512]{2,1,0:T(8,128)(2,1)} %vol_in.1, bf16[27,32,64]{2,1,0:T(8,128)(2,1)} %bitcast.9, f32[1,64]{1,0:T(1,128)} %bitcast.10, bf16[27,64,128]{2,1,0:T(8,128)(2,1)} %bitcast.8, f32[1,128]{1,0:T(1,128)} %bitcast.11, ...), custom_call_target="tpu_custom_call" | custom-call | tf_op jit(solution)/shard_map/step/pallas_call | solution.py:567
  67.4 2.4 %finish.1 = (bf16[1,128,1024]{2,1,0:T(8,128)(2,1)}, f32[27,32,64]{2,1,0:T(8,128)}, f32[27,64,128]{2,1,0:T(8,128)}, f32[1,64]{1,0:T(1,128)}, f32[1,128]{1,0:T(1,128)}) custom-call(bf16[128,1024]{1,0:T(8,128)(2,1)} %get-tuple-element.13.feat_in, f32[8,7,8,128]{3,2,1,0:T(8,128)} %get-tuple-element.14.c1_in, bf16[8,14,16,128]{3,2,1,0:T(8,128)(2,1)} %get-tuple-element.15.c2_in), custom_call_target="tpu_custom_call" | custom-call | tf_op jit(solution)/shard_map/finish/pallas_call | solution.py:617
